TPU v7x, 128 devices: a whole 4x4x4 slice. The times are simulated.
128 devices in a mesh: row: 8 (over y, core), col: 16 (over x, z).
Axes of the slice: x: 4, y: 4, z: 4, core: 2. Of those that a mesh axis runs over, the one named last changes fastest.
Arguments:
- b_tensor: bfloat16 [128, 1024, 1024], P('col', 'row'), may hold values from -6 to 6
- occ_green: bfloat16 [1024, 1024], P(('row', 'col')), may hold values from -0.1875 to 0.1875
- virt_green: bfloat16 [1024, 1024], P(('row', 'col')), may hold values from -0.1875 to 0.1875
- b_mask: int32 [1, 8, 8], replicated, may hold values 0 or 1
- occ_mask: int32 [8, 8], replicated, may hold values 0 or 1
- virt_mask: int32 [8, 8], replicated, may hold values 0 or 1
Outputs:
- chi: float32 [128, 128], P(('row', 'col'))
All inputs are finite; a program needn't handle non-finite values.
Results may differ from a plain program's by a relative error of at most 0.0041.
Values may be sent and summed in bfloat16 or wider, within the bound.
A program may use at most 64 MiB of HBM per device.

v0:
```python
import jax
import jax.numpy as jnp
from jax import lax
from jax.sharding import PartitionSpec as P

TILE = 128


def expand_pair(mask):
    return jnp.repeat(jnp.repeat(mask, TILE, axis=0), TILE, axis=1).astype(jnp.bfloat16)


def per_device(b_tensor, occ_green, virt_green, b_mask, occ_mask, virt_mask):
    col_index = lax.axis_index("col")
    row_index = lax.axis_index("row")
    p_count, m_count, n_basis = b_tensor.shape
    p_tiles = (col_index * p_count + jnp.arange(p_count, dtype=jnp.int32)) // TILE
    m_tiles = (row_index * m_count + jnp.arange(m_count, dtype=jnp.int32)) // TILE
    local_mask = jnp.take(jnp.take(b_mask, p_tiles, axis=0), m_tiles, axis=1).astype(jnp.bfloat16)
    masked = b_tensor * jnp.repeat(local_mask, TILE, axis=2)
    exchanged_b = lax.all_to_all(masked, "col", split_axis=2, concat_axis=0, tiled=True)
    virt_full = lax.all_gather(virt_green, ("row", "col"), axis=0, tiled=True) * expand_pair(
        virt_mask
    )
    occ_rows = lax.all_gather(occ_green, "col", axis=0, tiled=True)
    occ_rows = occ_rows * lax.dynamic_slice_in_dim(
        expand_pair(occ_mask), row_index * m_count, m_count, 0
    )
    inner = jnp.dot(masked.reshape(-1, n_basis), virt_full, preferred_element_type=jnp.float32)
    inner = inner.astype(jnp.bfloat16).reshape(masked.shape)
    outer = jnp.einsum(
        "lm,pms->pls",
        occ_rows,
        lax.all_gather(inner, "row", axis=1, tiled=True),
        preferred_element_type=jnp.float32,
    ).astype(jnp.bfloat16)
    moved = lax.all_to_all(outer, "col", split_axis=2, concat_axis=0, tiled=True)
    b_flat = exchanged_b.reshape(exchanged_b.shape[0], -1)
    y_flat = moved.reshape(moved.shape[0], -1)
    summed = lax.psum_scatter(
        lax.dot_general(
            y_flat, b_flat, (((1,), (1,)), ((), ())), preferred_element_type=jnp.float32
        ),
        ("row", "col"),
        scatter_dimension=0,
        tiled=True,
    )
    return summed * (-2.0 / n_basis)


def solution(mesh):
    return jax.shard_map(
        per_device,
        mesh=mesh,
        in_specs=(
            P("col", "row", None),
            P(("row", "col"), None),
            P(("row", "col"), None),
            P(),
            P(),
            P(),
        ),
        out_specs=P(("row", "col"), None),
        check_vma=False,
    )
```

profile of v0, /device:TPU:1, one launch (start us, length us, event | category | flops | bytes accessed | tf_op | source)
XLA Modules:
  0.0 387.0 jit_solution(18253904898014795396)
XLA Ops:
  6.5 0.0 all-gather.3.cloned.1.call-start
  6.5 0.7 all-gather.3.cloned.1.call-update
  7.3 0.0 all-gather.5.cloned.1.call-start
  7.4 0.8 broadcast_select_fusion
  8.1 0.8 gather_fusion
  8.9 0.2 fusion.3
  9.2 1.4 broadcast_in_dim.39
  10.5 0.0 copy-start.1
  10.5 2.3 reshape.157
  12.8 0.0 copy-done.1
  12.8 3.2 mul.24
  16.1 63.1 %all-gather.3.cloned.1.call-done = bf16[1024,1024]{1,0:T(8,128)(2,1)} async-done(((bf16[8,1024]{1,0:T(8,128)(2,1)}), bf16[1024,1024]{1,0:T(8,128)(2,1)}) %all-gather.3.cloned.1.call-update) | async-done | bytes 2097168 | tf_op jit(solution)/shard_map/all_gather | solution.py:22
  79.2 0.0 copy-start.3
  79.3 2.9 broadcast_in_dim.41
  82.2 0.0 copy-done.3
  82.2 3.7 fusion.2
  85.9 3.9 %copy.19 = bf16[8,128,1024]{1,2,0:T(8,128)(2,1)} copy(bf16[8,128,1024]{2,1,0:T(8,128)(2,1)} %bitcast.45) | data formatting | bytes 4194304 | tf_op jit(solution)/shard_map/reshape | solution.py:30
  89.8 0.0 all-gather.5.cloned.1.call-update
  89.9 2.9 copy.22
  92.8 0.0 copy-start.2
  92.8 4.2 %all-to-all-start.1 = ((bf16[8,128,1024]{1,0,2:T(8,128)(2,1)}), bf16[8,128,1024]{1,0,2:T(8,128)(2,1)S(1)}, u32[]{:S(2)}, u32[]{:S(2)}) async-start(bf16[8,128,1024]{1,0,2:T(8,128)(2,1)} %copy.22), calls=%async_computation.1 | async-start | bytes 4194304 | tf_op jit(solution)/shard_map/all_to_all | solution.py:21
  97.0 0.0 copy-done.2
  97.1 2.9 broadcast_in_dim.43
  100.0 0.0 copy-start
  100.1 2.0 copy.35
  102.0 0.0 copy-done
  102.0 36.4 %all_gather.11 = bf16[128,1024]{1,0:T(8,128)(2,1)S(1)} all-gather(bf16[8,1024]{1,0:T(8,128)(2,1)S(1)} %copy-done), channel_id=1, replica_groups=mesh['row'=8,'col'=16] {'col'}, dimensions={0}, use_global_device_ids=true | all-gather | bytes 278528 | tf_op jit(solution)/shard_map/all_gather | solution.py:25
  138.5 39.3 %all-gather.5.cloned.1.call-done = bf16[8,1024,1024]{1,2,0:T(8,128)(2,1)} async-done(((bf16[8,128,1024]{1,2,0:T(8,128)(2,1)}), bf16[8,1024,1024]{1,2,0:T(8,128)(2,1)}) %all-gather.5.cloned.1.call-update) | async-done | bytes 16777232 | tf_op jit(solution)/shard_map/all_gather | solution.py:34
  177.7 10.3 %convert_bitcast_fusion = bf16[8,128,1024]{1,2,0:T(8,128)(2,1)S(1)} fusion(bf16[8,1024,1024]{1,2,0:T(8,128)(2,1)} %all-gather.5.cloned.1.call-done, bf16[128,1024]{1,0:T(8,128)(2,1)S(1)} %all_gather.11, bf16[1024,1024]{1,0:T(8,128)(2,1)} %bitcast.44, s32[]{:T(128)S(6)} %select_n.83), kind=kOutput, calls=%fused_computation.5 | convolution fusion | flops 2149056512 | bytes 19398660 | tf_op jit(solution)/shard_map/lm,pms->pls/dot_general | solution.py:31
  188.0 2.7 copy.20
  190.7 0.0 all-to-all-done.1
  190.7 6.7 %all-to-all-start = ((bf16[8,128,1024]{1,0,2:T(8,128)(2,1)}), bf16[8,128,1024]{1,0,2:T(8,128)(2,1)}, u32[]{:S(2)}, u32[]{:S(2)}) async-start(bf16[8,128,1024]{1,0,2:T(8,128)(2,1)} %copy.20), calls=%async_computation | async-start | bytes 4194304 | tf_op jit(solution)/shard_map/all_to_all | solution.py:37
  197.5 0.0 all-reduce.3.cloned.1.call-start
  197.5 3.2 copy.24
  200.7 5.7 %reshape.161 = bf16[128,8192]{1,0:T(8,128)(2,1)S(1)} reshape(bf16[16,8,128,64]{3,2,1,0:T(8,128)(2,1)} %copy.24) | data formatting | bytes 4194304 | tf_op jit(solution)/shard_map/reshape | solution.py:38
  206.4 20.3 %all-to-all-done = bf16[8,128,1024]{1,0,2:T(8,128)(2,1)} async-done(((bf16[8,128,1024]{1,0,2:T(8,128)(2,1)}), bf16[8,128,1024]{1,0,2:T(8,128)(2,1)}, u32[]{:S(2)}, u32[]{:S(2)}) %all-to-all-start) | async-done | bytes 2097184 | tf_op jit(solution)/shard_map/all_to_all | solution.py:37
  226.7 4.8 %copy.21 = bf16[8,128,16,64]{3,1,0,2:T(8,128)(2,1)} copy(bf16[8,128,16,64]{1,0,3,2:T(8,128)(2,1)} %bitcast.9) | data formatting | bytes 4194304 | tf_op jit(solution)/shard_map/all_to_all | solution.py:37
  231.5 6.6 %reshape.160 = bf16[128,8192]{1,0:T(8,128)(2,1)} reshape(bf16[16,8,128,64]{3,2,1,0:T(8,128)(2,1)} %bitcast.39) | data formatting | bytes 4194304 | tf_op jit(solution)/shard_map/reshape | solution.py:39
  238.1 2.9 fusion.9
  241.1 0.0 all-reduce.3.cloned.1.call-update
  241.1 138.1 %all-reduce.3.cloned.1.call-done = f32[128,128]{1,0:T(8,128)} async-done(((f32[128,128]{1,0:T(8,128)}), f32[128,128]{1,0:T(8,128)}) %all-reduce.3.cloned.1.call-update) | async-done | bytes 65552
  379.2 1.2 dynamic-slice_multiply_fusion
  (9 shorter events, 0.2 us)
Async XLA Ops:
  6.5 72.7 %all-gather.3.cloned.1.call-start = ((), (), s32[]{:S(2)}) async-start(), calls=%async_computation.2 | async-start | bytes 2113536 | tf_op jit(solution)/shard_map/all_gather | solution.py:22
  7.3 170.5 %all-gather.5.cloned.1.call-start = ((), (), s32[]{:S(2)}) async-start(), calls=%async_computation.3 | async-start | bytes 18874368 | tf_op jit(solution)/shard_map/all_gather | solution.py:34
  10.5 2.3 copy-start.1
  79.2 3.0 copy-start.3
  92.8 4.2 %copy-start.2 = (s32[8,8]{1,0:T(8,128)S(1)}, s32[8,8]{1,0:T(8,128)}, u32[]{:S(2)}) copy-start(s32[8,8]{1,0:T(8,128)} %param.10) | copy-start | bytes 772
  92.8 97.9 %all-to-all-start.1 = ((bf16[8,128,1024]{1,0,2:T(8,128)(2,1)}), bf16[8,128,1024]{1,0,2:T(8,128)(2,1)S(1)}, u32[]{:S(2)}, u32[]{:S(2)}) async-start(bf16[8,128,1024]{1,0,2:T(8,128)(2,1)} %copy.22), calls=%async_computation.1 | async-start | bytes 4194304 | tf_op jit(solution)/shard_map/all_to_all | solution.py:21
  100.0 2.0 copy-start
  190.7 36.0 %all-to-all-start = ((bf16[8,128,1024]{1,0,2:T(8,128)(2,1)}), bf16[8,128,1024]{1,0,2:T(8,128)(2,1)}, u32[]{:S(2)}, u32[]{:S(2)}) async-start(bf16[8,128,1024]{1,0,2:T(8,128)(2,1)} %copy.20), calls=%async_computation | async-start | bytes 4194304 | tf_op jit(solution)/shard_map/all_to_all | solution.py:37
  197.5 181.8 %all-reduce.3.cloned.1.call-start = ((), (), s32[]{:S(2)}) async-start(), calls=%async_computation.4 | async-start | bytes 131072
Sparse Core Ops, SparseCore 0:
  10.3 68.8 all-gather.2
  90.0 87.6 all-gather.4
  241.2 137.9 all-reduce.2
where the time goes:
time: 388 us; the launch traced here: 387 us
  waiting for transfers between devices  262 us (68%)
  local copies, waits for them, and re-layouts  42.2 us (11%)
  blocking collectives  36.4 us (9%)
  matrix products  16.9 us (4%)
  between operations  13.3 us (3%)
  starting transfers between devices  11 us (3%)
  other arithmetic  5.47 us (1%)
    unnamed x4, waiting for transfers between devices  139 us
    all_gather x1, waiting for transfers between devices, per_device(): lax.all_gather(virt_green, ('row', 'col'), axis=0, tiled=True)  63.1 us
    all_gather x1, waiting for transfers between devices, per_device(): lax.all_gather(inner, 'row', axis=1, tiled=True)  39.3 us
    all_gather x1, blocking collectives, per_device(): occ_rows = lax.all_gather(occ_green, 'col', axis=0, tiled=True)  36.4 us
    all_to_all x1, waiting for transfers between devices, per_device(): lax.all_to_all(outer, 'col', split_axis=2, concat_axis=0, tiled=True)  20.3 us
    dot_general x1, matrix products, per_device(): jnp.einsum('lm,pms->pls', occ_rows, lax.all_gather(inner, 'row', axis=1,...  10.3 us
  transfers between devices with their start and end apart: 5, of which 4 were waited for; matrix products, arithmetic and copies ran while one was open for 10% of the time, Pallas kernels for 0%

commit v1 on v0

--- a/solution.py
+++ b/solution.py
@@ -22,7 +22,9 @@
     virt_full = lax.all_gather(virt_green, ("row", "col"), axis=0, tiled=True) * expand_pair(
         virt_mask
     )
-    occ_rows = lax.all_gather(occ_green, "col", axis=0, tiled=True)
+    occ_rows = jnp.concatenate(
+        lax.all_to_all(jnp.stack([occ_green] * lax.axis_size("col")), "col", 0, 0), axis=0
+    )
     occ_rows = occ_rows * lax.dynamic_slice_in_dim(
         expand_pair(occ_mask), row_index * m_count, m_count, 0
     )

time: 388 us -> 388 us (level)
  blocking collectives: 36.4 us -> 0 us
  waiting for transfers between devices: 262 us -> 293 us
    all_gather x1 -> x0, blocking collectives: 36.4 us -> none  [per_device(): occ_rows = lax.all_gather(occ_green, 'col', axis=0, tiled=True)]
    all_gather x1, waiting for transfers between devices: 39.3 us -> 65.7 us  [per_device(): lax.all_gather(inner, 'row', axis=1, tiled=True)]
    all_to_all x0 -> x1, waiting for transfers between devices: none -> 4.78 us  [per_device(): lax.all_to_all(jnp.stack([occ_green] * lax.axis_size('col')), 'col', 0, 0)]
    all_to_all x0 -> x1, starting transfers between devices: none -> 4.09 us  [per_device(): lax.all_to_all(jnp.stack([occ_green] * lax.axis_size('col')), 'col', 0, 0)]
  transfers between devices with their start and end apart: 5 -> 6, of which waited for: 4 -> 5; matrix products, arithmetic and copies ran while one was open for 10% -> 10% of each run, Pallas kernels for 0% -> 0%
where the time goes in v1:
time: 388 us; the launch traced here: 387 us
  waiting for transfers between devices  293 us (76%)
  local copies, waits for them, and re-layouts  43.8 us (11%)
  matrix products  16.9 us (4%)
  starting transfers between devices  14.8 us (4%)
  between operations  13.3 us (3%)
  other arithmetic  5.46 us (1%)
    unnamed x4, waiting for transfers between devices  139 us
    all_gather x1, waiting for transfers between devices, per_device(): lax.all_gather(inner, 'row', axis=1, tiled=True)  65.7 us
    all_gather x1, waiting for transfers between devices, per_device(): lax.all_gather(virt_green, ('row', 'col'), axis=0, tiled=True)  63.1 us
    all_to_all x1, waiting for transfers between devices, per_device(): lax.all_to_all(outer, 'col', split_axis=2, concat_axis=0, tiled=True)  20.3 us
    dot_general x1, matrix products, per_device(): jnp.einsum('lm,pms->pls', occ_rows, lax.all_gather(inner, 'row', axis=1,...  10.3 us
  transfers between devices with their start and end apart: 6, of which 5 were waited for; matrix products, arithmetic and copies ran while one was open for 10% of the time, Pallas kernels for 0%

profile of v1, /device:TPU:1, one launch (start us, length us, event | category | flops | bytes accessed | tf_op | source)
XLA Modules:
  0.0 387.0 jit_solution(13422273665811436567)
XLA Ops:
  6.5 0.0 all-gather.3.cloned.1.call-start
  6.5 0.7 all-gather.3.cloned.1.call-update
  7.3 0.0 all-gather.5.cloned.1.call-start
  7.4 0.8 broadcast_select_fusion
  8.1 0.8 gather_fusion
  8.9 0.2 fusion.3
  9.2 1.4 broadcast_in_dim.39
  10.5 0.0 copy-start.1
  10.5 2.3 reshape.162
  12.9 0.0 copy-done.1
  12.9 3.2 mul.24
  16.1 63.1 %all-gather.3.cloned.1.call-done = bf16[1024,1024]{1,0:T(8,128)(2,1)} async-done(((bf16[8,1024]{1,0:T(8,128)(2,1)}), bf16[1024,1024]{1,0:T(8,128)(2,1)}) %all-gather.3.cloned.1.call-update) | async-done | bytes 2097168 | tf_op jit(solution)/shard_map/all_gather | solution.py:22
  79.2 0.0 copy-start.3
  79.3 2.9 broadcast_in_dim.41
  82.2 0.0 copy-done.3
  82.2 3.7 fusion.2
  85.9 3.9 %copy.19 = bf16[8,128,1024]{1,2,0:T(8,128)(2,1)} copy(bf16[8,128,1024]{2,1,0:T(8,128)(2,1)} %bitcast.50) | data formatting | bytes 4194304 | tf_op jit(solution)/shard_map/reshape | solution.py:32
  89.9 0.0 copy-start
  89.9 0.0 all-gather.5.cloned.1.call-update
  89.9 0.7 copy-done
  90.6 0.7 stack.2
  91.3 4.1 %all-to-all-start = ((bf16[16,8,1024]{2,1,0:T(8,128)(2,1)}), bf16[16,8,1024]{2,1,0:T(8,128)(2,1)S(1)}, u32[]{:S(2)}, u32[]{:S(2)}) async-start(bf16[16,8,1024]{2,1,0:T(8,128)(2,1)} %stack.2), calls=%async_computation | async-start | bytes 524288 | tf_op jit(solution)/shard_map/all_to_all | solution.py:26
  95.4 2.9 copy.22
  98.3 0.0 copy-start.2
  98.3 4.8 %all-to-all-done = bf16[16,8,1024]{2,1,0:T(8,128)(2,1)S(1)} async-done(((bf16[16,8,1024]{2,1,0:T(8,128)(2,1)}), bf16[16,8,1024]{2,1,0:T(8,128)(2,1)S(1)}, u32[]{:S(2)}, u32[]{:S(2)}) %all-to-all-start) | async-done | bytes 262176 | tf_op jit(solution)/shard_map/all_to_all | solution.py:26
  103.1 3.9 %all-to-all-start.2 = ((bf16[8,128,1024]{1,0,2:T(8,128)(2,1)}), bf16[8,128,1024]{1,0,2:T(8,128)(2,1)S(1)}, u32[]{:S(2)}, u32[]{:S(2)}) async-start(bf16[8,128,1024]{1,0,2:T(8,128)(2,1)} %copy.22), calls=%async_computation.2 | async-start | bytes 4194304 | tf_op jit(solution)/shard_map/all_to_all | solution.py:21
  107.0 0.0 copy-done.2
  107.1 2.9 broadcast_in_dim.43
  110.1 2.0 copy.35
  112.0 65.7 %all-gather.5.cloned.1.call-done = bf16[8,1024,1024]{1,2,0:T(8,128)(2,1)} async-done(((bf16[8,128,1024]{1,2,0:T(8,128)(2,1)}), bf16[8,1024,1024]{1,2,0:T(8,128)(2,1)}) %all-gather.5.cloned.1.call-update) | async-done | bytes 16777232 | tf_op jit(solution)/shard_map/all_gather | solution.py:36
  177.7 10.3 %convert_bitcast_fusion = bf16[8,128,1024]{1,2,0:T(8,128)(2,1)S(1)} fusion(bf16[8,1024,1024]{1,2,0:T(8,128)(2,1)} %all-gather.5.cloned.1.call-done, bf16[16,8,1024]{2,1,0:T(8,128)(2,1)S(1)} %all-to-all-done, bf16[1024,1024]{1,0:T(8,128)(2,1)} %bitcast.49, s32[]{:T(128)S(6)} %select_n.83), kind=kOutput, calls=%fused_computation.5 | convolution fusion | flops 2149056512 | bytes 19398660 | tf_op jit(solution)/shard_map/lm,pms->pls/dot_general | solution.py:33
  188.1 2.7 copy.20
  190.8 0.0 all-to-all-done.2
  190.8 6.7 %all-to-all-start.1 = ((bf16[8,128,1024]{1,0,2:T(8,128)(2,1)}), bf16[8,128,1024]{1,0,2:T(8,128)(2,1)}, u32[]{:S(2)}, u32[]{:S(2)}) async-start(bf16[8,128,1024]{1,0,2:T(8,128)(2,1)} %copy.20), calls=%async_computation.1 | async-start | bytes 4194304 | tf_op jit(solution)/shard_map/all_to_all | solution.py:39
  197.5 0.0 all-reduce.3.cloned.1.call-start
  197.5 3.2 copy.24
  200.8 5.7 %reshape.167 = bf16[128,8192]{1,0:T(8,128)(2,1)S(1)} reshape(bf16[16,8,128,64]{3,2,1,0:T(8,128)(2,1)} %copy.24) | data formatting | bytes 4194304 | tf_op jit(solution)/shard_map/reshape | solution.py:40
  206.4 20.3 %all-to-all-done.1 = bf16[8,128,1024]{1,0,2:T(8,128)(2,1)} async-done(((bf16[8,128,1024]{1,0,2:T(8,128)(2,1)}), bf16[8,128,1024]{1,0,2:T(8,128)(2,1)}, u32[]{:S(2)}, u32[]{:S(2)}) %all-to-all-start.1) | async-done | bytes 2097184 | tf_op jit(solution)/shard_map/all_to_all | solution.py:39
  226.7 4.8 %copy.21 = bf16[8,128,16,64]{3,1,0,2:T(8,128)(2,1)} copy(bf16[8,128,16,64]{1,0,3,2:T(8,128)(2,1)} %bitcast.10) | data formatting | bytes 4194304 | tf_op jit(solution)/shard_map/all_to_all | solution.py:39
  231.6 6.6 %reshape.166 = bf16[128,8192]{1,0:T(8,128)(2,1)} reshape(bf16[16,8,128,64]{3,2,1,0:T(8,128)(2,1)} %bitcast.44) | data formatting | bytes 4194304 | tf_op jit(solution)/shard_map/reshape | solution.py:41
  238.2 2.9 fusion.8
  241.1 0.0 all-reduce.3.cloned.1.call-update
  241.1 138.2 %all-reduce.3.cloned.1.call-done = f32[128,128]{1,0:T(8,128)} async-done(((f32[128,128]{1,0:T(8,128)}), f32[128,128]{1,0:T(8,128)}) %all-reduce.3.cloned.1.call-update) | async-done | bytes 65552
  379.3 1.2 dynamic-slice_multiply_fusion
  (9 shorter events, 0.2 us)
Async XLA Ops:
  6.5 72.7 %all-gather.3.cloned.1.call-start = ((), (), s32[]{:S(2)}) async-start(), calls=%async_computation.3 | async-start | bytes 2113536 | tf_op jit(solution)/shard_map/all_gather | solution.py:22
  7.3 170.5 %all-gather.5.cloned.1.call-start = ((), (), s32[]{:S(2)}) async-start(), calls=%async_computation.4 | async-start | bytes 18874368 | tf_op jit(solution)/shard_map/all_gather | solution.py:36
  10.5 2.3 copy-start.1
  79.2 3.0 copy-start.3
  89.9 0.7 copy-start
  91.3 11.8 %all-to-all-start = ((bf16[16,8,1024]{2,1,0:T(8,128)(2,1)}), bf16[16,8,1024]{2,1,0:T(8,128)(2,1)S(1)}, u32[]{:S(2)}, u32[]{:S(2)}) async-start(bf16[16,8,1024]{2,1,0:T(8,128)(2,1)} %stack.2), calls=%async_computation | async-start | bytes 524288 | tf_op jit(solution)/shard_map/all_to_all | solution.py:26
  98.3 8.7 %copy-start.2 = (s32[8,8]{1,0:T(8,128)S(1)}, s32[8,8]{1,0:T(8,128)}, u32[]{:S(2)}) copy-start(s32[8,8]{1,0:T(8,128)} %param.10) | copy-start | bytes 772
  103.1 87.6 %all-to-all-start.2 = ((bf16[8,128,1024]{1,0,2:T(8,128)(2,1)}), bf16[8,128,1024]{1,0,2:T(8,128)(2,1)S(1)}, u32[]{:S(2)}, u32[]{:S(2)}) async-start(bf16[8,128,1024]{1,0,2:T(8,128)(2,1)} %copy.22), calls=%async_computation.2 | async-start | bytes 4194304 | tf_op jit(solution)/shard_map/all_to_all | solution.py:21
  190.8 36.0 %all-to-all-start.1 = ((bf16[8,128,1024]{1,0,2:T(8,128)(2,1)}), bf16[8,128,1024]{1,0,2:T(8,128)(2,1)}, u32[]{:S(2)}, u32[]{:S(2)}) async-start(bf16[8,128,1024]{1,0,2:T(8,128)(2,1)} %copy.20), calls=%async_computation.1 | async-start | bytes 4194304 | tf_op jit(solution)/shard_map/all_to_all | solution.py:39
  197.5 181.8 %all-reduce.3.cloned.1.call-start = ((), (), s32[]{:S(2)}) async-start(), calls=%async_computation.5 | async-start | bytes 131072
Sparse Core Ops, SparseCore 0:
  10.3 68.8 all-gather.2
  90.0 87.6 all-gather.4
  241.3 138.0 all-reduce.2
